TPU v7x, 512 devices: a whole 4x4x16 slice. The times are simulated.
512 devices in a mesh: coef: 16 (over z_lo, y), pair: 32 (over z_hi, x, core).
Axes of the slice: x: 4, y: 4, z: 16 (z_hi: 4, z_lo: 4; z = z_hi * 4 + z_lo), core: 2. Of those that a mesh axis runs over, the one named last changes fastest.
Arguments:
- integrals: bfloat16 [2048, 32, 8192], P(('coef', 'pair')), may hold values from -66 to 66
- coefficients: bfloat16 [2, 8192, 384], P(None, ('coef', 'pair')), may hold values from -0.0625 to 0.0625
- shell_starts: int32 [8], replicated, may hold values from 0 to 8188, as said below
- pair_ids: int32 [16, 128], P('coef'), may hold values from 0 to 127, each once within a row
Outputs:
- half_ints: bfloat16 [2, 384, 384, 2048], P(None, 'pair', None, 'coef')
Inputs may be any that keep to these rules, and one draw needn't show every extreme that they name: `shell_starts`: distinct multiples of 4.
All inputs are finite; a program needn't handle non-finite values.
Results may differ from a plain program's by a relative error of at most 0.0049.
Values may be sent and summed in bfloat16 or wider, within the bound.
A program may use at most 64 MiB of HBM per device.

v0:
```python
import jax
import jax.numpy as jnp
from jax import lax
from jax.sharding import PartitionSpec as P

SHW = 4


def on_device(integrals, coefficients, shell_starts, pair_ids):
    slot_count, batch_rows, ao_width = integrals.shape
    occupied = coefficients.shape[2]
    flat_ints = integrals.reshape(slot_count * batch_rows, ao_width)
    offsets = jnp.arange(SHW, dtype=jnp.int32)
    batch_index = (shell_starts[:, None] + offsets[None, :]).reshape(-1)
    panel_piece = lax.all_gather(coefficients, ("coef", "pair"), axis=1, tiled=True)
    products = jnp.einsum("rn,cnj->crj", flat_ints, panel_piece, preferred_element_type=jnp.float32)
    row_count = panel_piece.shape[1]
    inside_mask = (batch_index >= 0) & (batch_index < row_count)
    safe_index = jnp.clip(batch_index, 0, row_count - 1)
    chosen = jnp.take(panel_piece, safe_index, axis=1).astype(jnp.float32)
    picked = jnp.where(inside_mask[None, :, None], chosen, 0.0)
    half_done, picked = (products, picked)
    batch_coef = picked.astype(jnp.bfloat16)
    half_done = half_done.astype(jnp.bfloat16).reshape(2, slot_count, batch_rows, occupied)
    real_part = jnp.einsum(
        "mi,kmj->kij", batch_coef[0], half_done[0], preferred_element_type=jnp.float32
    ) + jnp.einsum("mi,kmj->kij", batch_coef[1], half_done[1], preferred_element_type=jnp.float32)
    imag_part = jnp.einsum(
        "mi,kmj->kij", batch_coef[0], half_done[1], preferred_element_type=jnp.float32
    ) - jnp.einsum("mi,kmj->kij", batch_coef[1], half_done[0], preferred_element_type=jnp.float32)
    local_block = jnp.stack([real_part, imag_part]).astype(jnp.bfloat16)
    arrived = lax.all_to_all(local_block, "pair", split_axis=2, concat_axis=1, tiled=True)
    pair_order = pair_ids.reshape(-1)
    columns = jnp.arange(pair_order.shape[0], dtype=jnp.int32)
    selector = (pair_order[:, None] == columns[None, :]).astype(jnp.bfloat16)
    result = jnp.einsum("csij,sq->cijq", arrived, selector, preferred_element_type=jnp.float32)
    return result.astype(jnp.bfloat16)


def solution(mesh):
    return jax.shard_map(
        on_device,
        mesh=mesh,
        in_specs=(
            P(("coef", "pair"), None, None),
            P(None, ("coef", "pair"), None),
            P(),
            P("coef", None),
        ),
        out_specs=P(None, "pair", None, "coef"),
        check_vma=False,
    )
```

profile of v0, /device:TPU:97, one launch (start us, length us, event | category | flops | bytes accessed | tf_op | source)
XLA Modules:
  0.0 1120.1 jit_solution(15795770854735174628)
XLA Ops:
  6.5 0.0 copy-start
  6.5 0.0 all-gather.2.cloned.1.call-start
  6.5 0.7 all-gather.2.cloned.1.call-update
  7.3 0.7 fusion.14
  8.0 0.1 min.18
  8.1 0.1 min.16
  8.1 0.7 fusion.17
  8.9 0.1 and.18
  9.0 832.1 %all-gather.2.cloned.1.call-done = bf16[2,8192,384]{2,1,0:T(8,128)(2,1)} async-done(((bf16[2,16,384]{2,1,0:T(8,128)(2,1)}), bf16[2,8192,384]{2,1,0:T(8,128)(2,1)}) %all-gather.2.cloned.1.call-update) | async-done | bytes 12582928 | tf_op jit(solution)/shard_map/all_gather | solution.py:15
  841.1 0.0 copy-done
  841.1 0.0 copy-start.1
  841.1 6.5 fusion.7
  847.7 1.6 copy-done.1
  849.3 117.8 %copy.11 = bf16[2,8192,384]{2,0,1:T(2,128)(2,1)} copy(bf16[2,8192,384]{2,1,0:T(8,128)(2,1)S(1)} %copy-done.1) | data formatting | bytes 25165824 | tf_op jit(solution)/shard_map/all_gather | solution.py:15
  967.0 5.2 gather_fusion
  972.3 0.1 fusion.10
  972.4 0.5 fusion.13
  972.9 0.5 fusion.12
  973.4 0.5 fusion.5
  973.9 0.5 fusion.6
  974.4 1.7 pad_maximum_fusion
  976.1 5.4 copy.13
  981.5 127.7 %all_to_all.18 = bf16[2,4,384,384]{3,1,0,2:T(4,128)(2,1)S(1)} all-to-all(bf16[2,4,384,384]{3,1,0,2:T(4,128)(2,1)} %copy.13), channel_id=1, replica_groups=mesh['coef'=16,'pair'=32] {'pair'}, dimensions={2} | all-to-all | bytes 4718592 | tf_op jit(solution)/shard_map/all_to_all | solution.py:32
  1109.1 0.0 copy-start.2
  1109.2 1.8 copy.15
  1111.0 0.0 copy-done.2
  1111.0 2.3 fusion.2
  (4 shorter events, 0.0 us)
Async XLA Ops:
  6.5 834.6 %copy-start = (bf16[4,32,8192]{2,1,0:T(8,128)(2,1)S(1)}, bf16[4,32,8192]{2,1,0:T(8,128)(2,1)}, u32[]{:S(2)}) copy-start(bf16[4,32,8192]{2,1,0:T(8,128)(2,1)} %param.4) | copy-start | bytes 6291460
  6.5 834.6 %all-gather.2.cloned.1.call-start = ((), (), s32[]{:S(2)}) async-start(), calls=%async_computation.1 | async-start | bytes 12607488 | tf_op jit(solution)/shard_map/all_gather | solution.py:15
  841.1 8.2 copy-start.1
  1109.1 1.8 copy-start.2
Sparse Core Ops, SparseCore 0:
  9.5 831.5 all-gather.1
where the time goes:
time: 1120 us
  waiting for transfers between devices  833 us (74%)
  local copies, waits for them, and re-layouts  132 us (12%)
  blocking collectives  128 us (11%)
  between operations  13.5 us (1%)
    all_gather x1, waiting for transfers between devices, on_device(): lax.all_gather(coefficients, ('coef', 'pair'), axis=1, tiled=True)  832 us
    all_to_all x1, blocking collectives, on_device(): lax.all_to_all(local_block, 'pair', split_axis=2, concat_axis=1, tiled=True)  128 us
    all_gather x1, local copies, waits for them, and re-layouts, on_device(): lax.all_gather(coefficients, ('coef', 'pair'), axis=1, tiled=True)  118 us
  transfers between devices with their start and end apart: 1, of which 1 were waited for; matrix products, arithmetic and copies ran while one was open for 0% of the time, Pallas kernels for 0%

commit v1 on v0

--- a/solution.py
+++ b/solution.py
@@ -1,3 +1,4 @@
+import functools
 import jax
 import jax.numpy as jnp
 from jax import lax
@@ -6,13 +7,21 @@
 SHW = 4
 
 
+def bench_read(payload, mesh_dim):
+    last = lax.all_to_all(jnp.stack(lax.axis_size(mesh_dim) * [payload]), mesh_dim, 0, 0)
+    return jnp.concatenate(last, axis=1)
+
+
+draft_map = functools.partial(bench_read, mesh_dim=("coef", "pair"))
+
+
 def on_device(integrals, coefficients, shell_starts, pair_ids):
     slot_count, batch_rows, ao_width = integrals.shape
     occupied = coefficients.shape[2]
     flat_ints = integrals.reshape(slot_count * batch_rows, ao_width)
     offsets = jnp.arange(SHW, dtype=jnp.int32)
     batch_index = (shell_starts[:, None] + offsets[None, :]).reshape(-1)
-    panel_piece = lax.all_gather(coefficients, ("coef", "pair"), axis=1, tiled=True)
+    panel_piece = draft_map(coefficients)
     products = jnp.einsum("rn,cnj->crj", flat_ints, panel_piece, preferred_element_type=jnp.float32)
     row_count = panel_piece.shape[1]
     inside_mask = (batch_index >= 0) & (batch_index < row_count)

time: 1120 us -> 844 us (0.75)
  the two profiles are of different devices: /device:TPU:97 before, /device:TPU:33 now
where the time goes in v1:
time: 844 us; the launch traced here: 843 us
  waiting for transfers between devices  541 us (64%)
  local copies, waits for them, and re-layouts  144 us (17%)
  blocking collectives  125 us (15%)
  starting transfers between devices  25.1 us (3%)
    all_to_all x1, waiting for transfers between devices, bench_read(): lax.all_to_all(jnp.stack(lax.axis_size(mesh_dim) * [payload]), mesh_dim,...  541 us
    reshape x2, local copies, waits for them, and re-layouts, bench_read(): return jnp.concatenate(last, axis=1)  125 us
    all_to_all x1, blocking collectives, on_device(): lax.all_to_all(local_block, 'pair', split_axis=2, concat_axis=1, tiled=True)  125 us
    all_to_all x1, starting transfers between devices, bench_read(): lax.all_to_all(jnp.stack(lax.axis_size(mesh_dim) * [payload]), mesh_dim,...  25.1 us
  transfers between devices with their start and end apart: 1, of which 1 were waited for; matrix products, arithmetic and copies ran while one was open for 0% of the time, Pallas kernels for 0%

profile of v1, /device:TPU:33, one launch (start us, length us, event | category | flops | bytes accessed | tf_op | source)
XLA Modules:
  0.0 843.2 jit_solution(5279647766179504817)
XLA Ops:
  0.0 0.0 copy-start
  0.0 6.4 stack.11
  6.4 0.0 copy-start.2
  6.4 25.1 %all-to-all-start = ((bf16[512,2,16,384]{3,2,1,0:T(8,128)(2,1)}), bf16[512,2,16,384]{3,2,1,0:T(8,128)(2,1)}, u32[]{:S(2)}, u32[]{:S(2)}) async-start(bf16[512,2,16,384]{3,2,1,0:T(8,128)(2,1)} %stack.11), calls=%async_computation | async-start | bytes 25165824 | tf_op jit(solution)/shard_map/all_to_all | solution.py:11
  31.6 0.0 copy-done.2
  31.6 0.1 fusion.14
  31.7 0.1 min.18
  31.8 0.1 min.16
  31.8 0.1 fusion.17
  31.9 0.1 and.18
  32.1 541.1 %all-to-all-done = bf16[512,2,16,384]{3,2,1,0:T(8,128)(2,1)} async-done(((bf16[512,2,16,384]{3,2,1,0:T(8,128)(2,1)}), bf16[512,2,16,384]{3,2,1,0:T(8,128)(2,1)}, u32[]{:S(2)}, u32[]{:S(2)}) %all-to-all-start) | async-done | bytes 12582944 | tf_op jit(solution)/shard_map/all_to_all | solution.py:11
  573.1 7.0 copy.11
  580.1 117.9 %copy.12 = bf16[2,8192,384]{2,0,1:T(2,128)(2,1)} copy(bf16[2,8192,384]{2,1,0:T(8,128)(2,1)S(1)} %bitcast.48) | data formatting | bytes 25165824 | tf_op jit(solution)/shard_map/reshape | solution.py:12
  698.0 0.0 copy-done
  698.0 1.9 fusion.7
  700.0 5.2 gather_fusion
  705.2 0.1 fusion.10
  705.3 0.5 fusion.13
  705.8 0.5 fusion.12
  706.3 0.5 fusion.5
  706.9 0.5 fusion.6
  707.4 1.7 pad_maximum_fusion
  709.0 5.5 copy.14
  714.5 124.6 %all_to_all.23 = bf16[2,4,384,384]{3,1,0,2:T(4,128)(2,1)S(1)} all-to-all(bf16[2,4,384,384]{3,1,0,2:T(4,128)(2,1)} %copy.14), channel_id=1, replica_groups=mesh['coef'=16,'pair'=32] {'pair'}, dimensions={2} | all-to-all | bytes 4718592 | tf_op jit(solution)/shard_map/all_to_all | solution.py:41
  839.1 0.0 copy-start.1
  839.1 1.8 copy.16
  840.9 0.0 copy-done.1
  841.0 2.3 fusion.2
  (4 shorter events, 0.0 us)
Async XLA Ops:
  0.0 698.0 %copy-start = (bf16[4,32,8192]{2,1,0:T(8,128)(2,1)S(1)}, bf16[4,32,8192]{2,1,0:T(8,128)(2,1)}, u32[]{:S(2)}) copy-start(bf16[4,32,8192]{2,1,0:T(8,128)(2,1)} %param.4) | copy-start | bytes 6291460
  6.4 25.2 %copy-start.2 = (s32[8]{0:T(128)S(1)}, s32[8]{0:T(128)}, u32[]{:S(2)}) copy-start(s32[8]{0:T(128)} %param.6) | copy-start | bytes 100
  6.4 566.7 %all-to-all-start = ((bf16[512,2,16,384]{3,2,1,0:T(8,128)(2,1)}), bf16[512,2,16,384]{3,2,1,0:T(8,128)(2,1)}, u32[]{:S(2)}, u32[]{:S(2)}) async-start(bf16[512,2,16,384]{3,2,1,0:T(8,128)(2,1)} %stack.11), calls=%async_computation | async-start | bytes 25165824 | tf_op jit(solution)/shard_map/all_to_all | solution.py:11
  839.1 1.8 copy-start.1
